TPU v7x, 512 devices: a whole 4x4x16 slice. The times are simulated.
512 devices in a mesh: tok: 64 (over y_lo, z, core), head: 8 (over x, y_hi).
Axes of the slice: x: 4, y: 4 (y_hi: 2, y_lo: 2; y = y_hi * 2 + y_lo), z: 16, core: 2. Of those that a mesh axis runs over, the one named last changes fastest.
Arguments:
- query_rows: bfloat16 [16384, 40, 128], P('tok', 'head'), as said below
- key_rows: bfloat16 [16384, 40, 128], P('tok', 'head'), as said below
- value_rows: bfloat16 [16384, 40, 128], P('tok', 'head'), may hold values from -6 to 6
- query_gain: float32 [40, 128], P('head'), may hold values from 1.5 to 4
- key_gain: float32 [40, 128], P('head'), may hold values from 0.25 to 1.75
- rate_in: float32 [40, 16384], P('head', 'tok'), may hold values from 0.05 to 0.5
- rate_out: float32 [40, 16384], P('head', 'tok'), may hold values from 0.0002 to 0.002
- fast_in: bfloat16 [40, 128, 512], P('head'), may hold values from -6 to 6
- fast_out: bfloat16 [40, 256, 128], P('head'), may hold values from -0.375 to 0.375
- half_window: int32 [40], P('head'), may hold values from 128 to 1024, as said below
- boundaries: int32 [3], replicated, may hold values from 2049 to 16383, as said below
Outputs:
- layer_out: bfloat16 [16384, 40, 128], P('tok', 'head')
Inputs may be any that keep to these rules, and one draw needn't show every extreme that they name: `half_window`: no head sees more than 1024 tokens on either side; some head has exactly 1024 and some head exactly 128. `boundaries`: non-decreasing; the first is 2049 and the last 16383. `query_rows`: entries within -400 and 400. `key_rows`: entries within -400 and 400.
All inputs are finite; a program needn't handle non-finite values.
Results may differ from a plain program's by a relative error of at most 0.02.
Values may be sent and summed in bfloat16 or wider, within the bound.
A program may use at most 64 MiB of HBM per device.

v0:
```python
import math

import jax
import jax.numpy as jnp
from jax import lax
from jax.sharding import PartitionSpec as P

HALF = 1024


epsilon = 1e-06


def passed_along(x, axis, by):
    peers = lax.axis_size(axis)
    pairs = [(i, i + by) for i in range(peers) if 0 <= i + by < peers]
    return lax.ppermute(x, axis, pairs)


def unit_rows(matrix):
    as_float = matrix.astype(jnp.float32)
    return (
        as_float * lax.rsqrt(jnp.sum(as_float * as_float, axis=-1, keepdims=True) + epsilon)
    ).astype(jnp.bfloat16)


def rescale(updated, base_norm, squares):
    return (updated * (base_norm / jnp.sqrt(squares + epsilon))[:, None, :]).astype(jnp.bfloat16)


def body(
    query_rows,
    key_rows,
    value_rows,
    query_gain,
    key_gain,
    rate_in,
    rate_out,
    fast_in,
    fast_out,
    half_window,
    boundaries,
):
    tok_rows = query_rows.shape[0]
    local_heads = query_rows.shape[1]
    head_dim = query_rows.shape[2]
    fast_hid = fast_out.shape[1]
    width_all = local_heads * head_dim * lax.axis_size("head")
    tok_count = tok_rows * lax.axis_size("tok")
    own_index = lax.axis_index("tok")
    first_row = own_index * tok_rows
    query_float = query_rows.astype(jnp.float32)
    key_float = key_rows.astype(jnp.float32)
    query_sq, key_sq = lax.psum(
        (
            jnp.sum(query_float * query_float, axis=(1, 2)),
            jnp.sum(key_float * key_float, axis=(1, 2)),
        ),
        "head",
    )
    q_normed = (
        query_float * lax.rsqrt(query_sq / width_all + epsilon)[:, None, None] * query_gain[None]
    ).astype(jnp.bfloat16)
    k_normed = (
        key_float * lax.rsqrt(key_sq / width_all + epsilon)[:, None, None] * key_gain[None]
    ).astype(jnp.bfloat16)

    def clip_of(places):
        return jnp.sum((places[:, None] >= boundaries[None, :]).astype(jnp.int32), axis=1)

    positions = first_row + jnp.arange(tok_rows, dtype=jnp.int32)
    query_clip = clip_of(positions)
    scaling = 1.0 / math.sqrt(head_dim)

    def absorb(state_now, block_keys, block_values, key_first):
        best, denominator, accum = state_now
        key_places = key_first + jnp.arange(tok_rows, dtype=jnp.int32)
        scores = (
            jnp.einsum("qhd,khd->hqk", q_normed, block_keys, preferred_element_type=jnp.float32)
            * scaling
        )
        inside = (key_places >= 0) & (key_places < tok_count)
        pair_ok = (query_clip[:, None] == clip_of(key_places)[None, :]) & inside[None, :]
        distance = jnp.abs(positions[:, None] - key_places[None, :])
        allowed = (distance[None, :, :] <= half_window[:, None, None]) & pair_ok[None, :, :]
        masked = jnp.where(allowed, scores, -jnp.inf)
        new_best = jnp.maximum(best, jnp.max(masked, axis=2))
        weights = jnp.exp(masked - new_best[:, :, None])
        shrink = jnp.exp(best - new_best)
        denominator = denominator * shrink + jnp.sum(weights, axis=2)
        accum = accum * shrink[:, :, None] + jnp.einsum(
            "hqk,khd->hqd",
            weights.astype(jnp.bfloat16),
            block_values,
            preferred_element_type=jnp.float32,
        )
        return (new_best, denominator, accum)

    start_state = (
        jnp.full((local_heads, tok_rows), -jnp.inf, jnp.float32),
        jnp.zeros((local_heads, tok_rows), jnp.float32),
        jnp.zeros((local_heads, tok_rows, head_dim), jnp.float32),
    )
    state_now = absorb(start_state, k_normed, value_rows, first_row)
    reach_blocks = HALF // tok_rows
    for distance_step in range(1, reach_blocks + 1):
        left_keys, left_values = passed_along((k_normed, value_rows), "tok", distance_step)
        state_now = absorb(state_now, left_keys, left_values, first_row - distance_step * tok_rows)
        right_keys, right_values = passed_along((k_normed, value_rows), "tok", -distance_step)
        state_now = absorb(
            state_now, right_keys, right_values, first_row + distance_step * tok_rows
        )
    attended = state_now[2] / state_now[1][:, :, None]
    key_unit = unit_rows(k_normed)
    query_unit = unit_rows(q_normed)
    pre_keys = jnp.einsum("thd,hdf->htf", key_unit, fast_in, preferred_element_type=jnp.float32)
    gate_part = pre_keys[:, :, :fast_hid]
    lin_part = pre_keys[:, :, fast_hid:]
    sigmoid_gate = jax.nn.sigmoid(gate_part)
    swish_gate = gate_part * sigmoid_gate
    hidden = (swish_gate * lin_part).astype(jnp.bfloat16)
    value_float = value_rows.astype(jnp.float32)
    push_out = (-jnp.transpose(rate_out)[:, :, None] * value_float).astype(jnp.bfloat16)
    push_in = (-jnp.transpose(rate_in)[:, :, None] * value_float).astype(jnp.bfloat16)
    grad_out = jnp.einsum("htf,thd->hfd", hidden, push_out, preferred_element_type=jnp.float32)
    hidden_grad = jnp.einsum("thd,hfd->htf", push_in, fast_out, preferred_element_type=jnp.float32)
    d_gate = hidden_grad * lin_part * sigmoid_gate * (1.0 + gate_part * (1.0 - sigmoid_gate))
    d_lin = hidden_grad * swish_gate
    d_pre = jnp.concatenate([d_gate, d_lin], axis=2).astype(jnp.bfloat16)
    grad_in = jnp.einsum("thd,htf->hdf", key_unit, d_pre, preferred_element_type=jnp.float32)
    in_float = fast_in.astype(jnp.float32)
    out_float = fast_out.astype(jnp.float32)
    in_base = jnp.sqrt(jnp.sum(in_float * in_float, axis=1))
    out_base = jnp.sqrt(jnp.sum(out_float * out_float, axis=1))
    summed_in, summed_out = lax.psum((grad_in, grad_out), "tok")
    updated_in = in_float - summed_in
    updated_out = out_float - summed_out
    new_in = rescale(updated_in, in_base, jnp.sum(updated_in * updated_in, axis=1))
    new_out = rescale(updated_out, out_base, jnp.sum(updated_out * updated_out, axis=1))
    pre_query = jnp.einsum("thd,hdf->htf", query_unit, new_in, preferred_element_type=jnp.float32)
    query_gate = pre_query[:, :, :fast_hid]
    query_hidden = (query_gate * jax.nn.sigmoid(query_gate) * pre_query[:, :, fast_hid:]).astype(
        jnp.bfloat16
    )
    fast_result = jnp.einsum(
        "htf,hfd->htd", query_hidden, new_out, preferred_element_type=jnp.float32
    )
    combined = attended + fast_result
    return jnp.transpose(combined, (1, 0, 2)).astype(jnp.bfloat16)


def solution(mesh):
    in_specs = (
        P("tok", "head", None),
        P("tok", "head", None),
        P("tok", "head", None),
        P("head", None),
        P("head", None),
        P("head", "tok"),
        P("head", "tok"),
        P("head", None, None),
        P("head", None, None),
        P("head"),
        P(),
    )
    out_specs = P("tok", "head", None)
    return jax.shard_map(body, mesh=mesh, in_specs=in_specs, out_specs=out_specs, check_vma=False)
```

profile of v0, /device:TPU:1, one launch (start us, length us, event | category | flops | bytes accessed | tf_op | source)
XLA Modules:
  0.0 515.0 jit_solution(13826565609350189376)
XLA Ops:
  6.5 1.3 fusion.54
  7.9 21.4 %all-reduce.1 = (f32[256]{0:T(256)S(1)}, f32[256]{0:T(256)S(1)}) all-reduce(f32[256]{0:T(256)S(1)} %get-tuple-element.83, f32[256]{0:T(256)S(1)} %get-tuple-element.82), channel_id=1, replica_groups=mesh['tok'=64,'head'=8] {'head'}, use_global_device_ids=true, to_apply=%region_4.0 | all-reduce | flops 512 | bytes 4096 | tf_op jit(solution)/shard_map/psum | solution.py:54
  29.3 1.3 fusion.62
  30.6 1.3 collective-permute-start.14
  31.9 6.3 %collective-permute-start.12 = (bf16[256,5,128]{2,0,1:T(8,128)(2,1)S(1)}, bf16[256,5,128]{2,0,1:T(8,128)(2,1)}, u32[]{:S(2)}, u32[]{:S(2)}) collective-permute-start(bf16[256,5,128]{2,0,1:T(8,128)(2,1)S(1)} %get-tuple-element.42), channel_id=1, source_target_pairs={{0,32},{8,40},{16,48},{24,56},{32,64},{40,72},{48,80},{56,88},{64,... | collective-permute-start | bytes 983048 | tf_op jit(solution)/shard_map/ppermute | solution.py:17
  38.2 1.3 collective-permute-start.10
  39.5 10.6 %collective-permute-start.8 = (bf16[256,5,128]{2,0,1:T(8,128)(2,1)S(1)}, bf16[256,5,128]{2,0,1:T(8,128)(2,1)S(1)}, u32[]{:S(2)}, u32[]{:S(2)}) collective-permute-start(bf16[256,5,128]{2,0,1:T(8,128)(2,1)S(1)} %get-tuple-element.42), channel_id=1, source_target_pairs={{0,24},{8,32},{16,40},{24,48},{32,56},{40,64},{48,72},{56,80},{64,... | collective-permute-start | bytes 983048 | tf_op jit(solution)/shard_map/ppermute | solution.py:17
  50.1 1.3 collective-permute-start.6
  52.3 2.5 fusion.77
  54.7 1.9 multiply_convert_fusion.3
  56.6 1.9 fusion.11
  61.5 4.2 collective-permute-start.4
  65.7 1.5 fusion.130
  67.3 1.9 collective-permute-start.2
  69.2 1.5 fusion.131
  70.8 3.6 collective-permute-start
  75.0 1.9 collective-permute-start.3
  77.5 3.7 collective-permute-start.5
  81.7 1.3 collective-permute-start.7
  83.6 7.2 %collective-permute-start.9 = (bf16[256,5,128]{2,0,1:T(8,128)(2,1)}, bf16[256,5,128]{2,0,1:T(8,128)(2,1)S(1)}, u32[]{:S(2)}, u32[]{:S(2)}) collective-permute-start(bf16[256,5,128]{2,0,1:T(8,128)(2,1)} %param.13), channel_id=1, source_target_pairs={{0,24},{8,32},{16,40},{24,48},{32,56},{40,64},{48,72},{56,80},{64,... | collective-permute-start | bytes 983048 | tf_op jit(solution)/shard_map/ppermute | solution.py:17
  91.4 1.3 collective-permute-start.11
  93.9 9.0 %collective-permute-start.13 = (bf16[256,5,128]{2,0,1:T(8,128)(2,1)}, bf16[256,5,128]{2,0,1:T(8,128)(2,1)S(1)}, u32[]{:S(2)}, u32[]{:S(2)}) collective-permute-start(bf16[256,5,128]{2,0,1:T(8,128)(2,1)} %param.13), channel_id=1, source_target_pairs={{0,32},{8,40},{16,48},{24,56},{32,64},{40,72},{48,80},{56,88},{64,... | collective-permute-start | bytes 983048 | tf_op jit(solution)/shard_map/ppermute | solution.py:17
  103.7 1.5 collective-permute-start.15
  106.4 2.2 collective-permute-start.1
  110.3 1.3 convolution_bitcast_fusion.4
  111.5 1.3 convolution_bitcast_fusion.3
  113.0 1.3 convolution_bitcast_fusion.2
  114.3 9.1 %collective-permute-done.15 = bf16[256,5,128]{2,0,1:T(8,128)(2,1)S(1)} collective-permute-done((bf16[256,5,128]{2,0,1:T(8,128)(2,1)}, bf16[256,5,128]{2,0,1:T(8,128)(2,1)S(1)}, u32[]{:S(2)}, u32[]{:S(2)}) %collective-permute-start.15) | collective-permute-done | bytes 327712 | tf_op jit(solution)/shard_map/ppermute | solution.py:17
  124.6 2.5 fusion.18
  127.2 372.7 %all-reduce.4.cloned.1.call-done = (f32[5,128,512]{2,1,0:T(8,128)}, f32[5,256,128]{2,1,0:T(8,128)}) async-done(((f32[5,128,512]{2,1,0:T(8,128)}, f32[5,256,128]{2,1,0:T(8,128)}), (f32[5,128,512]{2,1,0:T(8,128)}, f32[5,256,128]{2,1,0:T(8,128)})) %all-reduce.4.cloned.1.call-update) | async-done | bytes 1966096 | tf_op jit(solution)/shard_map/psum | solution.py:135
  499.9 1.8 fusion.9
  505.0 3.2 fusion.35
  (102 shorter events, 16.0 us)
Async XLA Ops:
  6.5 44.9 %copy-start.14 = (f32[5,256]{1,0:T(8,128)S(1)}, f32[5,256]{1,0:T(8,128)}, u32[]{:S(2)}) copy-start(f32[5,256]{1,0:T(8,128)} %param.16) | copy-start | bytes 15364
  6.5 44.9 %copy-start.15 = (f32[5,256]{1,0:T(8,128)S(1)}, f32[5,256]{1,0:T(8,128)}, u32[]{:S(2)}) copy-start(f32[5,256]{1,0:T(8,128)} %param.17) | copy-start | bytes 15364
  6.5 44.9 %copy-start = (bf16[5,128,512]{2,1,0:T(8,128)(2,1)S(1)}, bf16[5,128,512]{2,1,0:T(8,128)(2,1)}, u32[]{:S(2)}) copy-start(bf16[5,128,512]{2,1,0:T(8,128)(2,1)} %param.18) | copy-start | bytes 1966084
  6.5 493.3 %all-reduce.4.cloned.1.call-start = ((), (), s32[]{:S(2)}) async-start(), calls=%async_computation | async-start | bytes 3932160 | tf_op jit(solution)/shard_map/psum | solution.py:135
  30.6 30.9 %collective-permute-start.14 = (bf16[256,5,128]{2,0,1:T(8,128)(2,1)S(1)}, bf16[256,5,128]{2,0,1:T(8,128)(2,1)}, u32[]{:S(2)}, u32[]{:S(2)}) collective-permute-start(bf16[256,5,128]{2,0,1:T(8,128)(2,1)S(1)} %get-tuple-element.42), channel_id=1, source_target_pairs={{32,0},{40,8},{48,16},{56,24},{64,32},{72,40},{80,48},{88,56},{96,... | collective-permute-start | bytes 983048 | tf_op jit(solution)/shard_map/ppermute | solution.py:17
  31.9 35.3 %collective-permute-start.12 = (bf16[256,5,128]{2,0,1:T(8,128)(2,1)S(1)}, bf16[256,5,128]{2,0,1:T(8,128)(2,1)}, u32[]{:S(2)}, u32[]{:S(2)}) collective-permute-start(bf16[256,5,128]{2,0,1:T(8,128)(2,1)S(1)} %get-tuple-element.42), channel_id=1, source_target_pairs={{0,32},{8,40},{16,48},{24,56},{32,64},{40,72},{48,80},{56,88},{64,... | collective-permute-start | bytes 983048 | tf_op jit(solution)/shard_map/ppermute | solution.py:17
  38.2 32.6 %collective-permute-start.10 = (bf16[256,5,128]{2,0,1:T(8,128)(2,1)S(1)}, bf16[256,5,128]{2,0,1:T(8,128)(2,1)S(1)}, u32[]{:S(2)}, u32[]{:S(2)}) collective-permute-start(bf16[256,5,128]{2,0,1:T(8,128)(2,1)S(1)} %get-tuple-element.42), channel_id=1, source_target_pairs={{24,0},{32,8},{40,16},{48,24},{56,32},{64,40},{72,48},{80,56},{88,... | collective-permute-start | bytes 983048 | tf_op jit(solution)/shard_map/ppermute | solution.py:17
  39.5 35.5 %collective-permute-start.8 = (bf16[256,5,128]{2,0,1:T(8,128)(2,1)S(1)}, bf16[256,5,128]{2,0,1:T(8,128)(2,1)S(1)}, u32[]{:S(2)}, u32[]{:S(2)}) collective-permute-start(bf16[256,5,128]{2,0,1:T(8,128)(2,1)S(1)} %get-tuple-element.42), channel_id=1, source_target_pairs={{0,24},{8,32},{16,40},{24,48},{32,56},{40,64},{48,72},{56,80},{64,... | collective-permute-start | bytes 983048 | tf_op jit(solution)/shard_map/ppermute | solution.py:17
  50.1 27.3 %collective-permute-start.6 = (bf16[256,5,128]{2,0,1:T(8,128)(2,1)S(1)}, bf16[256,5,128]{2,0,1:T(8,128)(2,1)S(1)}, u32[]{:S(2)}, u32[]{:S(2)}) collective-permute-start(bf16[256,5,128]{2,0,1:T(8,128)(2,1)S(1)} %get-tuple-element.42), channel_id=1, source_target_pairs={{16,0},{24,8},{32,16},{40,24},{48,32},{56,40},{64,48},{72,56},{80,... | collective-permute-start | bytes 983048 | tf_op jit(solution)/shard_map/ppermute | solution.py:17
  52.3 2.5 copy-start.11
  58.7 2.1 copy-start.17
  61.5 20.2 %collective-permute-start.4 = (bf16[256,5,128]{2,0,1:T(8,128)(2,1)S(1)}, bf16[256,5,128]{2,0,1:T(8,128)(2,1)S(1)}, u32[]{:S(2)}, u32[]{:S(2)}) collective-permute-start(bf16[256,5,128]{2,0,1:T(8,128)(2,1)S(1)} %get-tuple-element.42), channel_id=1, source_target_pairs={{0,16},{8,24},{16,32},{24,40},{32,48},{40,56},{48,64},{56,72},{64,... | collective-permute-start | bytes 983048 | tf_op jit(solution)/shard_map/ppermute | solution.py:17
  67.3 16.3 %collective-permute-start.2 = (bf16[256,5,128]{2,0,1:T(8,128)(2,1)S(1)}, bf16[256,5,128]{2,0,1:T(8,128)(2,1)S(1)}, u32[]{:S(2)}, u32[]{:S(2)}) collective-permute-start(bf16[256,5,128]{2,0,1:T(8,128)(2,1)S(1)} %get-tuple-element.42), channel_id=1, source_target_pairs={{8,0},{16,8},{24,16},{32,24},{40,32},{48,40},{56,48},{64,56},{72,6... | collective-permute-start | bytes 983048 | tf_op jit(solution)/shard_map/ppermute | solution.py:17
  70.8 20.6 %collective-permute-start = (bf16[256,5,128]{2,0,1:T(8,128)(2,1)S(1)}, bf16[256,5,128]{2,0,1:T(8,128)(2,1)S(1)}, u32[]{:S(2)}, u32[]{:S(2)}) collective-permute-start(bf16[256,5,128]{2,0,1:T(8,128)(2,1)S(1)} %get-tuple-element.42), channel_id=1, source_target_pairs={{0,8},{8,16},{16,24},{24,32},{32,40},{40,48},{48,56},{56,64},{64,7... | collective-permute-start | bytes 983048 | tf_op jit(solution)/shard_map/ppermute | solution.py:17
  75.0 18.9 %collective-permute-start.3 = (bf16[256,5,128]{2,0,1:T(8,128)(2,1)}, bf16[256,5,128]{2,0,1:T(8,128)(2,1)S(1)}, u32[]{:S(2)}, u32[]{:S(2)}) collective-permute-start(bf16[256,5,128]{2,0,1:T(8,128)(2,1)} %param.13), channel_id=1, source_target_pairs={{8,0},{16,8},{24,16},{32,24},{40,32},{48,40},{56,48},{64,56},{72,6... | collective-permute-start | bytes 983048 | tf_op jit(solution)/shard_map/ppermute | solution.py:17
  77.5 26.2 %collective-permute-start.5 = (bf16[256,5,128]{2,0,1:T(8,128)(2,1)}, bf16[256,5,128]{2,0,1:T(8,128)(2,1)S(1)}, u32[]{:S(2)}, u32[]{:S(2)}) collective-permute-start(bf16[256,5,128]{2,0,1:T(8,128)(2,1)} %param.13), channel_id=1, source_target_pairs={{0,16},{8,24},{16,32},{24,40},{32,48},{40,56},{48,64},{56,72},{64,... | collective-permute-start | bytes 983048 | tf_op jit(solution)/shard_map/ppermute | solution.py:17
  81.7 24.7 %collective-permute-start.7 = (bf16[256,5,128]{2,0,1:T(8,128)(2,1)}, bf16[256,5,128]{2,0,1:T(8,128)(2,1)S(1)}, u32[]{:S(2)}, u32[]{:S(2)}) collective-permute-start(bf16[256,5,128]{2,0,1:T(8,128)(2,1)} %param.13), channel_id=1, source_target_pairs={{16,0},{24,8},{32,16},{40,24},{48,32},{56,40},{64,48},{72,56},{80,... | collective-permute-start | bytes 983048 | tf_op jit(solution)/shard_map/ppermute | solution.py:17
  83.6 26.7 %collective-permute-start.9 = (bf16[256,5,128]{2,0,1:T(8,128)(2,1)}, bf16[256,5,128]{2,0,1:T(8,128)(2,1)S(1)}, u32[]{:S(2)}, u32[]{:S(2)}) collective-permute-start(bf16[256,5,128]{2,0,1:T(8,128)(2,1)} %param.13), channel_id=1, source_target_pairs={{0,24},{8,32},{16,40},{24,48},{32,56},{40,64},{48,72},{56,80},{64,... | collective-permute-start | bytes 983048 | tf_op jit(solution)/shard_map/ppermute | solution.py:17
  91.4 20.1 %collective-permute-start.11 = (bf16[256,5,128]{2,0,1:T(8,128)(2,1)}, bf16[256,5,128]{2,0,1:T(8,128)(2,1)S(1)}, u32[]{:S(2)}, u32[]{:S(2)}) collective-permute-start(bf16[256,5,128]{2,0,1:T(8,128)(2,1)} %param.13), channel_id=1, source_target_pairs={{24,0},{32,8},{40,16},{48,24},{56,32},{64,40},{72,48},{80,56},{88,... | collective-permute-start | bytes 983048 | tf_op jit(solution)/shard_map/ppermute | solution.py:17
  93.9 19.1 %collective-permute-start.13 = (bf16[256,5,128]{2,0,1:T(8,128)(2,1)}, bf16[256,5,128]{2,0,1:T(8,128)(2,1)S(1)}, u32[]{:S(2)}, u32[]{:S(2)}) collective-permute-start(bf16[256,5,128]{2,0,1:T(8,128)(2,1)} %param.13), channel_id=1, source_target_pairs={{0,32},{8,40},{16,48},{24,56},{32,64},{40,72},{48,80},{56,88},{64,... | collective-permute-start | bytes 983048 | tf_op jit(solution)/shard_map/ppermute | solution.py:17
  103.7 19.7 %collective-permute-start.15 = (bf16[256,5,128]{2,0,1:T(8,128)(2,1)}, bf16[256,5,128]{2,0,1:T(8,128)(2,1)S(1)}, u32[]{:S(2)}, u32[]{:S(2)}) collective-permute-start(bf16[256,5,128]{2,0,1:T(8,128)(2,1)} %param.13), channel_id=1, source_target_pairs={{32,0},{40,8},{48,16},{56,24},{64,32},{72,40},{80,48},{88,56},{96,... | collective-permute-start | bytes 983048 | tf_op jit(solution)/shard_map/ppermute | solution.py:17
  106.4 397.0 %collective-permute-start.1 = (bf16[256,5,128]{2,0,1:T(8,128)(2,1)}, bf16[256,5,128]{2,0,1:T(8,128)(2,1)S(1)}, u32[]{:S(2)}, u32[]{:S(2)}) collective-permute-start(bf16[256,5,128]{2,0,1:T(8,128)(2,1)} %param.13), channel_id=1, source_target_pairs={{0,8},{8,16},{16,24},{24,32},{32,40},{40,48},{48,56},{56,64},{64,7... | collective-permute-start | bytes 983048 | tf_op jit(solution)/shard_map/ppermute | solution.py:17
  499.9 1.8 copy-start.10
  499.9 1.8 copy-start.12
  499.9 2.0 copy-start.1
  502.7 1.1 copy-start.3
  502.7 1.3 copy-start.4
  502.8 1.5 copy-start.5
  502.8 1.7 copy-start.6
  502.8 1.8 copy-start.7
  502.8 2.0 copy-start.8
  502.8 2.2 copy-start.9
  (3 other events, 2.6 us)
Sparse Core Ops, SparseCore 0:
  58.6 441.1 all-reduce.3
where the time goes:
time: 517 us; the launch traced here: 515 us
  waiting for transfers between devices  382 us (74%)
  starting transfers between devices  58.6 us (11%)
  matrix products  28.9 us (6%)
  blocking collectives  21.4 us (4%)
  between operations  14.1 us (3%)
  other arithmetic  8.21 us (2%)
    psum x1, waiting for transfers between devices, body(): summed_in, summed_out = lax.psum((grad_in, grad_out), 'tok')  373 us
    ppermute x16, starting transfers between devices, passed_along(): return lax.ppermute(x, axis, pairs)  58.6 us
    psum x1, blocking collectives, body(): lax.psum((jnp.sum(query_float * query_float, axis=(1, 2)), jnp.sum(key_fl...  21.4 us
    dot_general x9, matrix products, absorb(): jnp.einsum('hqk,khd->hqd', weights.astype(jnp.bfloat16), block_values, pr...  13.6 us
  transfers between devices with their start and end apart: 17, of which 2 were waited for; matrix products, arithmetic and copies ran while one was open for 6% of the time, Pallas kernels for 0%

commit v1 on v0

v1 whole, which is shorter than its diff:
```python
import math

import jax
import jax.numpy as jnp
from jax import lax
from jax.experimental import pallas as pl
from jax.experimental.pallas import tpu as pltpu
from jax.sharding import PartitionSpec as P

epsilon = 1e-06
MESH = pl.DeviceIdType.MESH
NEG = -1e30
GRAD_ROWS = 4096


def rows_to_columns(row, lanes):
    return jnp.transpose(jnp.broadcast_to(row, (lanes, row.shape[1])))


def silu_parts(gate):
    sigmoid = 1.0 / (1.0 + jnp.exp(-gate))
    return sigmoid, gate * sigmoid


def dot(a, b, dims=((1,), (0,))):
    return lax.dot_general(a, b, (dims, ((), ())), preferred_element_type=jnp.float32)


def kernel(
    heads_all,
    n_tok,
    n_head,
    q_ref,
    k_ref,
    v_ref,
    qg_ref,
    kg_ref,
    ri_ref,
    ro_ref,
    fi_ref,
    fo_ref,
    hw_ref,
    bd_ref,
    out_ref,
    kh,
    vh,
    ss_loc,
    ss_all,
    tot_all,
    qt,
    qu,
    m_ref,
    l_ref,
    acc,
    grad,
    rc,
    s1,
    ry,
    qb,
    rz,
    wsum,
    fast,
    ss_send,
    ss_recv,
    tot_send,
    tot_recv,
    hk_send,
    hk_recv,
    hv_send,
    hv_recv,
    rc_sem,
    ry_sem,
    rz_send,
    rz_recv,
    az_send,
    az_recv,
    ay_sem,
    ac_sem,
):
    local_heads, rows, dim = k_ref.shape
    hid = fo_ref.shape[1]
    total_tokens = rows * n_tok
    chips = n_tok // 2
    nz = chips // 2
    part = GRAD_ROWS // (4 * nz)
    t = lax.axis_index("tok")
    me_head = lax.axis_index("head")
    core = t % 2
    chip = t // 2
    z = chip % nz
    yl = chip // nz
    partner = t + 1 - 2 * core
    y_peer = (1 - yl) * (2 * nz) + z * 2 + core

    def z_peer(i):
        return yl * (2 * nz) + ((z + i) % nz) * 2 + core

    def tok_ring(off):
        return (t + off + n_tok) % n_tok

    def at_tok(dev):
        return (dev, me_head)

    barrier = pltpu.get_barrier_semaphore()

    def greet(dev):
        pl.semaphore_signal(barrier, inc=1, device_id=dev, device_id_type=MESH)

    for off in (1, 2, 3, 4):
        greet(at_tok(tok_ring(off)))
        greet(at_tok(tok_ring(-off)))
    for i in range(1, n_head):
        greet((t, (me_head + i) % n_head))
    for i in range(1, nz):
        greet(at_tok(z_peer(i)))
    greet(at_tok(y_peer))
    pl.semaphore_wait(barrier, 8 + (n_head - 1) + (nz - 1) + 1)

    def remote(src, dst, send, recv, dev):
        return pltpu.make_async_remote_copy(
            src_ref=src,
            dst_ref=dst,
            send_sem=send,
            recv_sem=recv,
            device_id=dev,
            device_id_type=MESH,
        )

    def halo(ref, buf, send, recv, slot, dev):
        return remote(ref, buf.at[slot], send.at[slot], recv.at[slot], at_tok(dev))

    near = ((1, tok_ring(2)), (2, tok_ring(-2)))
    far = ((0, tok_ring(4)), (3, tok_ring(-4)))
    k_copy = {}
    v_copy = {}
    for slot, dev in near + far:
        k_copy[slot] = halo(k_ref, kh, hk_send, hk_recv, slot, dev)
        v_copy[slot] = halo(v_ref, vh, hv_send, hv_recv, slot, dev)
    far_src = 3 * (1 - core)
    for slot, src in ((4, 1), (6, 2), (7, far_src)):
        k_copy[slot] = halo(kh.at[src], kh, hk_send, hk_recv, slot, partner)
        v_copy[slot] = halo(vh.at[src], vh, hv_send, hv_recv, slot, partner)
    k_copy[5] = halo(k_ref, kh, hk_send, hk_recv, 5, partner)
    v_copy[5] = halo(v_ref, vh, hv_send, hv_recv, 5, partner)
    side = 1 - 2 * core
    slot_off = {0: -4, 1: -2, 2: 2, 3: 4, 4: side - 2, 5: side, 6: side + 2, 7: -3 * side}

    for slot, _ in near:
        k_copy[slot].start()
    k_copy[5].start()
    v_copy[5].start()

    k_sq = jnp.zeros((rows, dim), jnp.float32)
    q_sq = jnp.zeros((rows, dim), jnp.float32)
    for h in range(local_heads):
        kf = k_ref[h].astype(jnp.float32)
        qf = q_ref[h].astype(jnp.float32)
        k_sq = k_sq + kf * kf
        q_sq = q_sq + qf * qf
    k_row = jnp.sum(jnp.transpose(k_sq), axis=0, keepdims=True)
    q_row = jnp.sum(jnp.transpose(q_sq), axis=0, keepdims=True)
    sub = lax.broadcasted_iota(jnp.int32, (8, rows), 0)
    ss_loc[...] = jnp.where(
        sub == 0, jnp.broadcast_to(k_row, (8, rows)), jnp.broadcast_to(q_row, (8, rows))
    )

    def ss_copy(i):
        other = (me_head + i) % n_head
        return remote(
            ss_loc, ss_all.at[me_head], ss_send.at[other], ss_recv.at[me_head], (t, other)
        )

    def ss_arrival(i):
        other = (me_head + i) % n_head
        return remote(
            ss_loc, ss_all.at[other], ss_send.at[other], ss_recv.at[other], (t, other)
        )

    for i in range(1, n_head):
        ss_copy(i).start()
    total = ss_loc[...]
    for i in range(1, n_head):
        ss_arrival(i).wait_recv()
        total = total + ss_all[(me_head + i) % n_head]
    tot_all[4] = total

    def tot_copy(off):
        return remote(
            tot_all.at[4],
            tot_all.at[4 - off],
            tot_send.at[4 - off],
            tot_recv.at[4 - off],
            at_tok(tok_ring(off)),
        )

    offsets = (1, -1, 2, -2, 3, -3, 4, -4)
    for off in offsets:
        tot_copy(off).start()
    for slot, _ in near:
        v_copy[slot].start()

    inv_width = 1.0 / (heads_all * dim)

    def scale_of(sums_row):
        return rows_to_columns(lax.rsqrt(sums_row * inv_width + epsilon), dim)

    def normed(block, scale, gain):
        return (block.astype(jnp.float32) * scale * gain).astype(jnp.bfloat16)

    def unit(block):
        as_float = block.astype(jnp.float32)
        squares = jnp.sum(as_float * as_float, axis=1, keepdims=True)
        return (as_float * lax.rsqrt(squares + epsilon)).astype(jnp.bfloat16)

    k_scale = scale_of(total[0:1])
    q_scale = scale_of(total[1:2])

    pad_rows = GRAD_ROWS - local_heads * 6 * 128
    grad[pl.ds(GRAD_ROWS - pad_rows, pad_rows)] = jnp.zeros((pad_rows, dim), jnp.bfloat16)

    def grads(h, carry):
        key_unit = unit(normed(k_ref[h], k_scale, kg_ref[pl.ds(h, 1)]))
        pre = dot(key_unit, fi_ref[h])
        gate = pre[:, :hid]
        lin = pre[:, hid:]
        sigmoid, swish = silu_parts(gate)
        hidden = (swish * lin).astype(jnp.bfloat16)
        value = v_ref[h].astype(jnp.float32)
        push_out = (-rows_to_columns(ro_ref[pl.ds(h, 1)], dim) * value).astype(jnp.bfloat16)
        push_in = (-rows_to_columns(ri_ref[pl.ds(h, 1)], dim) * value).astype(jnp.bfloat16)
        grad_out = dot(hidden, push_out, ((0,), (0,)))
        hidden_grad = dot(push_in, fo_ref[h], ((1,), (1,)))
        d_gate = hidden_grad * lin * sigmoid * (1.0 + gate * (1.0 - sigmoid))
        d_lin = hidden_grad * swish
        first = h * 768
        for j, d_part in enumerate((d_gate, d_lin)):
            grad_in = dot(key_unit, d_part.astype(jnp.bfloat16), ((0,), (0,)))
            for half in range(2):
                start = pl.multiple_of(first + (2 * j + half) * 128, 128)
                grad[pl.ds(start, 128)] = grad_in[:, half * 128 : half * 128 + 128].astype(
                    jnp.bfloat16
                )
        start = pl.multiple_of(first + 512, 128)
        grad[pl.ds(start, 256)] = grad_out.astype(jnp.bfloat16)
        return carry

    lax.fori_loop(0, local_heads, grads, 0)

    half_rows = GRAD_ROWS // 2
    quarter = GRAD_ROWS // 4

    def half_at(which):
        return pl.multiple_of(which * half_rows, half_rows)

    rc_copy = remote(
        grad.at[pl.ds(half_at(1 - core), half_rows)],
        rc,
        rc_sem.at[0],
        rc_sem.at[1],
        at_tok(partner),
    )
    rc_copy.start()

    scaling = math.log2(math.e) / math.sqrt(dim)

    def queries(h, carry):
        raw = q_ref[h].astype(jnp.float32) * q_scale * qg_ref[pl.ds(h, 1)]
        qt[h] = jnp.transpose(raw * scaling).astype(jnp.bfloat16)
        qu[h] = unit(raw.astype(jnp.bfloat16))
        return carry

    lax.fori_loop(0, local_heads, queries, 0)

    positions = t * rows + lax.broadcasted_iota(jnp.int32, (1, rows), 1)
    clip_first = jnp.zeros((1, rows), jnp.int32)
    clip_last = jnp.full((1, rows), total_tokens - 1, jnp.int32)
    for b in range(bd_ref.shape[0]):
        edge = bd_ref[b]
        clip_first = jnp.where(positions >= edge, jnp.maximum(clip_first, edge), clip_first)
        clip_last = jnp.where(positions < edge, jnp.minimum(clip_last, edge - 1), clip_last)

    def absorb(keys, values, off, first=False):
        scale = k_scale if first else scale_of(tot_all[off + 4][0:1])
        places = (t + off) * rows + lax.broadcasted_iota(jnp.int32, (rows, rows), 0)

        def one(h, carry):
            window = hw_ref[h]
            low = jnp.maximum(positions - window, clip_first)
            high = jnp.minimum(positions + window, clip_last)
            block = normed(keys[h], scale, kg_ref[pl.ds(h, 1)])
            scores = dot(block, qt[h])
            scores = jnp.where((places >= low) & (places <= high), scores, NEG)
            best = jnp.max(scores, axis=0, keepdims=True)
            if not first:
                best_old = m_ref[pl.ds(h, 1)]
                best = jnp.maximum(best, best_old)
            weights = jnp.exp2(scores - best)
            denom = jnp.sum(weights, axis=0, keepdims=True)
            product = dot(values[h], weights.astype(jnp.bfloat16), ((0,), (0,)))
            if not first:
                shrink = jnp.exp2(best_old - best)
                denom = denom + l_ref[pl.ds(h, 1)] * shrink
                product = product + acc[h] * shrink
            m_ref[pl.ds(h, 1)] = best
            l_ref[pl.ds(h, 1)] = denom
            acc[h] = product
            return carry

        lax.fori_loop(0, local_heads, one, 0)

    def absorb_slot(slot):
        absorb(kh.at[slot], vh.at[slot], slot_off[slot])

    def arrived(slot):
        k_copy[slot].wait_recv()
        v_copy[slot].wait_recv()

    absorb(k_ref, v_ref, 0, first=True)

    rc_copy.wait_recv()

    def rows_of(ref, start, size):
        return ref[pl.ds(pl.multiple_of(start, size), size)].astype(jnp.float32)

    away = (1 - yl) * quarter
    for i in range(4):
        size = quarter // 4
        s1[pl.ds(i * size, size)] = (
            rows_of(grad, core * half_rows + away + i * size, size)
            + rows_of(rc, away + i * size, size)
        ).astype(jnp.bfloat16)
    ry_copy = remote(s1, ry, ry_sem.at[0], ry_sem.at[1], at_tok(y_peer))
    ry_copy.start()
    for off in offsets:
        tot_copy(off).wait_recv()
    arrived(5)
    absorb_slot(5)

    ry_copy.wait_recv()
    home = yl * quarter
    for i in range(4):
        size = quarter // 4
        qb[pl.ds(i * size, size)] = (
            rows_of(grad, core * half_rows + home + i * size, size)
            + rows_of(rc, home + i * size, size)
            + rows_of(ry, i * size, size)
        ).astype(jnp.bfloat16)

    def part_at(which):
        return pl.ds(pl.multiple_of(which * part, part), part)

    def rz_copy(i):
        other = (z + i) % nz
        return remote(
            qb.at[part_at(other)],
            rz.at[z],
            rz_send.at[other],
            rz_recv.at[z],
            at_tok(z_peer(i)),
        )

    def rz_arrival(i):
        other = (z + i) % nz
        return remote(
            qb.at[part_at(other)],
            rz.at[other],
            rz_send.at[other],
            rz_recv.at[other],
            at_tok(z_peer(i)),
        )

    for i in range(1, nz):
        rz_copy(i).start()
    for slot, _ in far:
        k_copy[slot].start()
        v_copy[slot].start()

    for slot in (1, 2):
        arrived(slot)
        k_copy[slot + (3 if slot == 1 else 4)].start()
        v_copy[slot + (3 if slot == 1 else 4)].start()
    absorb_slot(1)
    absorb_slot(2)

    summed = (
        rows_of(grad, core * half_rows + home + z * part, part)
        + rows_of(rc, home + z * part, part)
        + rows_of(ry, z * part, part)
    )
    for i in range(1, nz):
        rz_arrival(i).wait_recv()
        summed = summed + rz[(z + i) % nz].astype(jnp.float32)
    mine = core * half_rows + home

    def sum_at(which):
        return pl.ds(pl.multiple_of(mine + which * part, part), part)

    wsum[sum_at(z)] = summed.astype(jnp.bfloat16)

    def az_copy(i):
        other = (z + i) % nz
        return remote(
            wsum.at[sum_at(z)],
            wsum.at[sum_at(z)],
            az_send.at[other],
            az_recv.at[z],
            at_tok(z_peer(i)),
        )

    def az_arrival(i):
        other = (z + i) % nz
        return remote(
            wsum.at[sum_at(other)],
            wsum.at[sum_at(other)],
            az_send.at[other],
            az_recv.at[other],
            at_tok(z_peer(i)),
        )

    for i in range(1, nz):
        az_copy(i).start()

    arrived(4)
    absorb_slot(4)
    arrived(6)
    absorb_slot(6)

    for i in range(1, nz):
        az_arrival(i).wait_recv()
    quarter_at = pl.ds(pl.multiple_of(mine, quarter), quarter)
    other_quarter = pl.ds(pl.multiple_of(core * half_rows + away, quarter), quarter)
    ay_copy = remote(
        wsum.at[quarter_at], wsum.at[quarter_at], ay_sem.at[0], ay_sem.at[1], at_tok(y_peer)
    )
    ay_arrival = remote(
        wsum.at[other_quarter],
        wsum.at[other_quarter],
        ay_sem.at[0],
        ay_sem.at[1],
        at_tok(y_peer),
    )
    ay_copy.start()

    arrived(0)
    arrived(3)
    k_copy[7].start()
    v_copy[7].start()
    absorb_slot(0)

    ay_arrival.wait_recv()
    my_half = pl.ds(half_at(core), half_rows)
    other_half = pl.ds(half_at(1 - core), half_rows)
    ac_copy = remote(
        wsum.at[my_half], wsum.at[my_half], ac_sem.at[0], ac_sem.at[1], at_tok(partner)
    )
    ac_arrival = remote(
        wsum.at[other_half], wsum.at[other_half], ac_sem.at[0], ac_sem.at[1], at_tok(partner)
    )
    ac_copy.start()
    absorb_slot(3)
    arrived(7)
    absorb_slot(7)
    ac_arrival.wait_recv()

    def renewed(base, start, size):
        base = base.astype(jnp.float32)
        updated = base - wsum[pl.ds(pl.multiple_of(start, 128), size)].astype(jnp.float32)
        norm = jnp.sqrt(jnp.sum(base * base, axis=0, keepdims=True))
        squares = jnp.sum(updated * updated, axis=0, keepdims=True)
        return (updated * (norm / jnp.sqrt(squares + epsilon))).astype(jnp.bfloat16)

    def finish(h, carry):
        query_unit = qu[h]
        first = h * 768
        query_hidden = []
        for half in range(2):
            gate = dot(
                query_unit,
                renewed(fi_ref[h, :, half * 128 : half * 128 + 128], first + half * 128, 128),
            )
            lin = dot(
                query_unit,
                renewed(
                    fi_ref[h, :, hid + half * 128 : hid + half * 128 + 128],
                    first + 256 + half * 128,
                    128,
                ),
            )
            query_hidden.append((silu_parts(gate)[1] * lin).astype(jnp.bfloat16))
        new_out = renewed(fo_ref[h], first + 512, hid)
        result = dot(jnp.concatenate(query_hidden, axis=1), new_out)
        attended = jnp.transpose(acc[h] / l_ref[pl.ds(h, 1)])
        out_ref[h] = (attended + result).astype(jnp.bfloat16)
        return carry

    lax.fori_loop(0, local_heads, finish, 0)

    for i in range(1, n_head):
        ss_copy(i).wait_send()
    for off in offsets:
        tot_copy(off).wait_send()
    for slot in range(8):
        k_copy[slot].wait_send()
        v_copy[slot].wait_send()
    rc_copy.wait_send()
    ry_copy.wait_send()
    for i in range(1, nz):
        rz_copy(i).wait_send()
        az_copy(i).wait_send()
    ay_copy.wait_send()
    ac_copy.wait_send()


def body(q, k, v, q_gain, k_gain, rate_in, rate_out, fast_in, fast_out, half_window, boundaries):
    rows, heads, dim = q.shape
    n_tok = lax.axis_size("tok")
    n_head = lax.axis_size("head")
    nz = n_tok // 4
    part = GRAD_ROWS // (4 * nz)
    bf16 = jnp.bfloat16
    f32 = jnp.float32
    vmem = pl.BlockSpec(memory_space=pltpu.VMEM)
    smem = pl.BlockSpec(memory_space=pltpu.SMEM)
    dma = pltpu.SemaphoreType.DMA

    def call(*refs):
        kernel(heads * n_head, n_tok, n_head, *refs)

    result = pl.pallas_call(
        call,
        out_shape=jax.ShapeDtypeStruct((heads, rows, dim), bf16),
        in_specs=[vmem] * 9 + [smem] * 2,
        out_specs=vmem,
        scratch_shapes=[
            pltpu.VMEM((8, heads, rows, dim), bf16),
            pltpu.VMEM((8, heads, rows, dim), bf16),
            pltpu.VMEM((8, rows), f32),
            pltpu.VMEM((n_head, 8, rows), f32),
            pltpu.VMEM((9, 8, rows), f32),
            pltpu.VMEM((heads, dim, rows), bf16),
            pltpu.VMEM((heads, rows, dim), bf16),
            pltpu.VMEM((8, rows), f32),
            pltpu.VMEM((8, rows), f32),
            pltpu.VMEM((heads, dim, rows), f32),
            pltpu.VMEM((GRAD_ROWS, dim), bf16),
            pltpu.VMEM((GRAD_ROWS // 2, dim), bf16),
            pltpu.VMEM((GRAD_ROWS // 4, dim), bf16),
            pltpu.VMEM((GRAD_ROWS // 4, dim), bf16),
            pltpu.VMEM((GRAD_ROWS // 4, dim), bf16),
            pltpu.VMEM((nz, part, dim), bf16),
            pltpu.VMEM((GRAD_ROWS, dim), bf16),
            pltpu.VMEM((8, 128), f32),
            dma((n_head,)),
            dma((n_head,)),
            dma((9,)),
            dma((9,)),
            dma((8,)),
            dma((8,)),
            dma((8,)),
            dma((8,)),
            dma((2,)),
            dma((2,)),
            dma((nz,)),
            dma((nz,)),
            dma((nz,)),
            dma((nz,)),
            dma((2,)),
            dma((2,)),
        ],
        compiler_params=pltpu.CompilerParams(
            collective_id=0, has_side_effects=True, vmem_limit_bytes=60 * 1024 * 1024
        ),
    )(
        jnp.transpose(q, (1, 0, 2)),
        jnp.transpose(k, (1, 0, 2)),
        jnp.transpose(v, (1, 0, 2)),
        q_gain,
        k_gain,
        rate_in,
        rate_out,
        fast_in,
        fast_out,
        half_window,
        boundaries,
    )
    return jnp.transpose(result, (1, 0, 2))


def solution(mesh):
    in_specs = (
        P("tok", "head", None),
        P("tok", "head", None),
        P("tok", "head", None),
        P("head", None),
        P("head", None),
        P("head", "tok"),
        P("head", "tok"),
        P("head", None, None),
        P("head", None, None),
        P("head"),
        P(),
    )
    out_specs = P("tok", "head", None)
    return jax.shard_map(body, mesh=mesh, in_specs=in_specs, out_specs=out_specs, check_vma=False)
```

time: 517 us -> 105 us (0.20)
  waiting for transfers between devices: 382 us -> 0 us
  Pallas kernels: 0 us -> 101 us
  starting transfers between devices: 58.6 us -> 0 us
  matrix products: 28.9 us -> 0 us
  blocking collectives: 21.4 us -> 0 us
  between operations: 14.1 us -> 0.01 us
  other arithmetic: 8.21 us -> 0 us
    psum x1 -> x0, waiting for transfers between devices: 373 us -> none  [body(): summed_in, summed_out = lax.psum((grad_in, grad_out), 'tok')]
    pallas_call x0 -> x1, Pallas kernels: none -> 101 us  [body(): pl.pallas_call(call, out_shape=jax.ShapeDtypeStruct((heads, rows, dim), b...]
    ppermute x16 -> x0, starting transfers between devices: 58.6 us -> none  [passed_along(): return lax.ppermute(x, axis, pairs)]
    dot_general x24 -> x0, matrix products: 28.9 us -> none  [the longest x9 13.6 us: absorb(): jnp.einsum('hqk,khd->hqd', weights.astype(jnp.bfloat16), block_values, pr...]
    psum x1 -> x0, blocking collectives: 21.4 us -> none  [body(): lax.psum((jnp.sum(query_float * query_float, axis=(1, 2)), jnp.sum(key_fl...]
    ppermute x16 -> x0, waiting for transfers between devices: 9.16 us -> none  [passed_along(): return lax.ppermute(x, axis, pairs)]
    reduce_sum x15 -> x0, other arithmetic: 6.7 us -> none  [the longest x1 1.76 us: body(): in_base = jnp.sqrt(jnp.sum(in_float * in_float, axis=1))]
  transfers between devices with their start and end apart: 17 -> 0, of which waited for: 2 -> 0; matrix products, arithmetic and copies ran while one was open for 6% -> 0% of each run, Pallas kernels for 0% -> 0%
where the time goes in v1:
time: 105 us; the launch traced here: 103 us
  Pallas kernels  101 us (96%)
  local copies, waits for them, and re-layouts  1.72 us (2%)
    pallas_call x1, Pallas kernels, body(): pl.pallas_call(call, out_shape=jax.ShapeDtypeStruct((heads, rows, dim), b...  101 us

profile of v1, /device:TPU:1, one launch (start us, length us, event | category | flops | bytes accessed | tf_op | source)
XLA Modules:
  0.0 103.0 jit_solution(13103822400918757342)
XLA Ops:
  0.0 101.2 %shard_map.109 = bf16[5,256,128]{2,1,0:T(8,128)(2,1)} custom-call(bf16[5,256,128]{2,1,0:T(8,128)(2,1)} %bitcast.5, bf16[5,256,128]{2,1,0:T(8,128)(2,1)} %bitcast.6, bf16[5,256,128]{2,1,0:T(8,128)(2,1)} %bitcast.7, f32[5,128]{1,0:T(8,128)} %refs_3_.1, f32[5,128]{1,0:T(8,128)} %refs_4_.1, f32[5,256]{1,0:T(8,128)} %refs_5_.1, f32[5,256]{1,0:T(8,128)} %refs_6_.1, ...), custom_call_target="tpu_custom_call" | custom-call | tf_op jit(solution)/shard_map/pallas_call | solution.py:529
  101.2 1.7 %copy.13 = bf16[256,5,128]{2,0,1:T(8,128)(2,1)} copy(bf16[256,5,128]{2,0,1:T(8,128)(2,1)} %bitcast.4) | data formatting | bytes 655360

commit v2 on v1

v2 whole, which is shorter than its diff:
```python
import math

import jax
import jax.numpy as jnp
from jax import lax
from jax.experimental import pallas as pl
from jax.experimental.pallas import tpu as pltpu
from jax.sharding import PartitionSpec as P

epsilon = 1e-06
MESH = pl.DeviceIdType.MESH
NEG = -1e30
HEAD_ROWS = 768
EIGHTH = 512


def far_first(n):
    return sorted(range(1, n), key=lambda i: (-min(i, n - i), i))


def rows_to_columns(row, lanes):
    return jnp.transpose(jnp.broadcast_to(row, (lanes, row.shape[1])))


def silu_parts(gate):
    sigmoid = 1.0 / (1.0 + jnp.exp(-gate))
    return sigmoid, gate * sigmoid


def dot(a, b, dims=((1,), (0,))):
    return lax.dot_general(a, b, (dims, ((), ())), preferred_element_type=jnp.float32)


def kernel(
    heads_all,
    n_tok,
    n_head,
    q_ref,
    k_ref,
    v_ref,
    qg_ref,
    kg_ref,
    ri_ref,
    ro_ref,
    fi_ref,
    fo_ref,
    hw_ref,
    bd_ref,
    out_ref,
    kh,
    vh,
    ss_loc,
    ss_all,
    tot_all,
    qt,
    qu,
    m_ref,
    l_ref,
    acc,
    pre_ref,
    push_ref,
    hg_ref,
    grad,
    rc,
    s1,
    ry,
    s2,
    rp,
    qb,
    rz,
    wsum,
    fast,
    ss_send,
    ss_recv,
    tot_send,
    tot_recv,
    hk_send,
    hk_recv,
    hv_send,
    hv_recv,
    rc_send,
    rc_recv,
    ry_send,
    ry_recv,
    rp_send,
    rp_recv,
    rz_send,
    rz_recv,
    az_send,
    az_recv,
    ap_send,
    ap_recv,
    ay_send,
    ay_recv,
    ac_send,
    ac_recv,
):
    local_heads, rows, dim = k_ref.shape
    hid = fo_ref.shape[1]
    total_tokens = rows * n_tok
    chips = n_tok // 2
    nz = chips // 2
    owners = nz // 2
    part = EIGHTH // owners
    t = lax.axis_index("tok")
    me_head = lax.axis_index("head")
    core = t % 2
    chip = t // 2
    z = chip % nz
    yl = chip // nz
    zp = z % 2
    zo = z // 2
    partner = t + 1 - 2 * core
    y_peer = (1 - yl) * (2 * nz) + z * 2 + core
    pair = yl * (2 * nz) + (z + 1 - 2 * zp) * 2 + core

    def z_peer(i):
        return yl * (2 * nz) + (((zo + i) % owners) * 2 + zp) * 2 + core

    def tok_ring(off):
        return (t + off + n_tok) % n_tok

    def at_tok(dev):
        return (dev, me_head)

    barrier = pltpu.get_barrier_semaphore()

    def greet(dev):
        pl.semaphore_signal(barrier, inc=1, device_id=dev, device_id_type=MESH)

    for i in far_first(owners):
        greet(at_tok(z_peer(i)))
    for i in range(1, n_head):
        greet((t, (me_head + i) % n_head))
    for off in (1, 2, 3, 4):
        greet(at_tok(tok_ring(off)))
        greet(at_tok(tok_ring(-off)))
    greet(at_tok(y_peer))
    greet(at_tok(pair))

    def remote(src, dst, send, recv, dev):
        return pltpu.make_async_remote_copy(
            src_ref=src,
            dst_ref=dst,
            send_sem=send,
            recv_sem=recv,
            device_id=dev,
            device_id_type=MESH,
        )

    def halo(ref, buf, send, recv, slot, dev):
        return remote(ref, buf.at[slot], send.at[slot], recv.at[slot], at_tok(dev))

    k_copy = {}
    v_copy = {}
    far_src = 3 * (1 - core)
    routes = (
        (1, None, tok_ring(2)),
        (2, None, tok_ring(-2)),
        (0, 1, tok_ring(2)),
        (3, 2, tok_ring(-2)),
        (4, 1, partner),
        (5, None, partner),
        (6, 2, partner),
        (7, far_src, partner),
    )
    for slot, src, dev in routes:
        k_src = k_ref if src is None else kh.at[src]
        v_src = v_ref if src is None else vh.at[src]
        k_copy[slot] = halo(k_src, kh, hk_send, hk_recv, slot, dev)
        v_copy[slot] = halo(v_src, vh, hv_send, hv_recv, slot, dev)
    side = 1 - 2 * core
    slot_off = {0: -4, 1: -2, 2: 2, 3: 4, 4: side - 2, 5: side, 6: side + 2, 7: -3 * side}

    k_sq = jnp.zeros((rows, dim), jnp.float32)
    q_sq = jnp.zeros((rows, dim), jnp.float32)
    for h in range(local_heads):
        kf = k_ref[h].astype(jnp.float32)
        qf = q_ref[h].astype(jnp.float32)
        k_sq = k_sq + kf * kf
        q_sq = q_sq + qf * qf
    k_row = jnp.sum(jnp.transpose(k_sq), axis=0, keepdims=True)
    q_row = jnp.sum(jnp.transpose(q_sq), axis=0, keepdims=True)
    sub = lax.broadcasted_iota(jnp.int32, (8, rows), 0)
    ss_loc[...] = jnp.where(
        sub == 0, jnp.broadcast_to(k_row, (8, rows)), jnp.broadcast_to(q_row, (8, rows))
    )

    pl.semaphore_wait(barrier, (owners - 1) + (n_head - 1) + 8 + 2)

    def ss_copy(i):
        other = (me_head + i) % n_head
        return remote(
            ss_loc, ss_all.at[me_head], ss_send.at[other], ss_recv.at[me_head], (t, other)
        )

    def ss_arrival(i):
        other = (me_head + i) % n_head
        return remote(
            ss_loc, ss_all.at[other], ss_send.at[other], ss_recv.at[other], (t, other)
        )

    for i in range(1, n_head):
        ss_copy(i).start()
    for slot in (1, 2, 5):
        k_copy[slot].start()

    def early(h, carry):
        key_gained = k_ref[h].astype(jnp.float32) * kg_ref[pl.ds(h, 1)]
        pre_ref[h] = dot(key_gained.astype(jnp.bfloat16), fi_ref[h])
        value = v_ref[h].astype(jnp.float32)
        push_ref[h] = (-rows_to_columns(ro_ref[pl.ds(h, 1)], dim) * value).astype(jnp.bfloat16)
        push_in = (-rows_to_columns(ri_ref[pl.ds(h, 1)], dim) * value).astype(jnp.bfloat16)
        hg_ref[h] = dot(push_in, fo_ref[h], ((1,), (1,)))
        return carry

    lax.fori_loop(0, local_heads, early, 0)
    for i in range(1, n_head):
        ss_arrival(i).wait_recv()
    total = ss_loc[...]
    for i in range(1, n_head):
        total = total + ss_all[(me_head + i) % n_head]
    tot_all[4] = total

    def tot_copy(off):
        return remote(
            tot_all.at[4],
            tot_all.at[4 - off],
            tot_send.at[4 - off],
            tot_recv.at[4 - off],
            at_tok(tok_ring(off)),
        )

    offsets = (1, -1, 2, -2, 3, -3, 4, -4)
    for off in offsets:
        tot_copy(off).start()
    for slot in (1, 2, 5):
        v_copy[slot].start()

    inv_width = 1.0 / (heads_all * dim)

    def scale_of(sums_row):
        return rows_to_columns(lax.rsqrt(sums_row * inv_width + epsilon), dim)

    def normed(block, scale, gain):
        return (block.astype(jnp.float32) * scale * gain).astype(jnp.bfloat16)

    def unit(block):
        as_float = block.astype(jnp.float32)
        squares = jnp.sum(as_float * as_float, axis=1, keepdims=True)
        return (as_float * lax.rsqrt(squares + epsilon)).astype(jnp.bfloat16)

    k_scale = scale_of(total[0:1])
    q_scale = scale_of(total[1:2])

    def rc_copy(h):
        return remote(
            grad.at[h, pl.ds(pl.multiple_of((1 - core) * 384, 384), 384)],
            rc.at[h],
            rc_send.at[h],
            rc_recv.at[h],
            at_tok(partner),
        )

    def grads(h, carry):
        raw = k_ref[h].astype(jnp.float32) * kg_ref[pl.ds(h, 1)]
        squares = jnp.sum(raw * raw, axis=1, keepdims=True)
        factor = k_scale * lax.rsqrt(squares * (k_scale * k_scale) + epsilon)
        key_unit = (raw * factor).astype(jnp.bfloat16)
        pre = pre_ref[h] * factor[:, :1]
        gate = pre[:, :hid]
        lin = pre[:, hid:]
        sigmoid, swish = silu_parts(gate)
        hidden = (swish * lin).astype(jnp.bfloat16)
        hidden_grad = hg_ref[h]
        d_gate = hidden_grad * lin * sigmoid * (1.0 + gate * (1.0 - sigmoid))
        d_lin = hidden_grad * swish
        for j, d_part in enumerate((d_gate, d_lin)):
            grad_in = dot(key_unit, d_part.astype(jnp.bfloat16), ((0,), (0,)))
            for half in range(2):
                grad[h, pl.ds((2 * j + half) * 128, 128)] = grad_in[
                    :, half * 128 : half * 128 + 128
                ].astype(jnp.bfloat16)
        grad[h, pl.ds(512, 256)] = dot(hidden, push_ref[h], ((0,), (0,))).astype(jnp.bfloat16)
        rc_copy(h).start()
        return carry

    lax.fori_loop(0, local_heads, grads, 0)

    scaling = math.log2(math.e) / math.sqrt(dim)

    def queries(h, carry):
        raw = q_ref[h].astype(jnp.float32) * q_scale * qg_ref[pl.ds(h, 1)]
        qt[h] = jnp.transpose(raw * scaling).astype(jnp.bfloat16)
        qu[h] = unit(raw.astype(jnp.bfloat16))
        return carry

    lax.fori_loop(0, local_heads, queries, 0)

    positions = t * rows + lax.broadcasted_iota(jnp.int32, (1, rows), 1)
    clip_first = jnp.zeros((1, rows), jnp.int32)
    clip_last = jnp.full((1, rows), total_tokens - 1, jnp.int32)
    for b in range(bd_ref.shape[0]):
        edge = bd_ref[b]
        clip_first = jnp.where(positions >= edge, jnp.maximum(clip_first, edge), clip_first)
        clip_last = jnp.where(positions < edge, jnp.minimum(clip_last, edge - 1), clip_last)

    def absorb(keys, values, off, first=False):
        scale = k_scale if first else scale_of(tot_all[off + 4][0:1])
        places = (t + off) * rows + lax.broadcasted_iota(jnp.int32, (rows, rows), 0)

        def one(h, carry):
            window = hw_ref[h]
            low = jnp.maximum(positions - window, clip_first)
            high = jnp.minimum(positions + window, clip_last)
            block = normed(keys[h], scale, kg_ref[pl.ds(h, 1)])
            scores = dot(block, qt[h])
            scores = jnp.where((places >= low) & (places <= high), scores, NEG)
            best = jnp.max(scores, axis=0, keepdims=True)
            if not first:
                best_old = m_ref[pl.ds(h, 1)]
                best = jnp.maximum(best, best_old)
            weights = jnp.exp2(scores - best)
            denom = jnp.sum(weights, axis=0, keepdims=True)
            product = dot(values[h], weights.astype(jnp.bfloat16), ((0,), (0,)))
            if not first:
                shrink = jnp.exp2(best_old - best)
                denom = denom + l_ref[pl.ds(h, 1)] * shrink
                product = product + acc[h] * shrink
            m_ref[pl.ds(h, 1)] = best
            l_ref[pl.ds(h, 1)] = denom
            acc[h] = product
            return carry

        lax.fori_loop(0, local_heads, one, 0)

    def absorb_slot(slot):
        absorb(kh.at[slot], vh.at[slot], slot_off[slot])

    def arrived(slot):
        k_copy[slot].wait_recv()
        v_copy[slot].wait_recv()

    def rows_of(ref, h, start, size):
        return ref[h, pl.ds(pl.multiple_of(start, size), size)].astype(jnp.float32)

    def ry_copy(h):
        return remote(s1.at[h], ry.at[h], ry_send.at[h], ry_recv.at[h], at_tok(y_peer))

    def rp_copy(h):
        return remote(s2.at[h], rp.at[h], rp_send.at[h], rp_recv.at[h], at_tok(pair))

    def core_stage(h, carry):
        rc_copy(h).wait_recv()
        away = (1 - yl) * 192
        s1[h] = (rows_of(grad, h, core * 384 + away, 192) + rows_of(rc, h, away, 192)).astype(
            jnp.bfloat16
        )
        ry_copy(h).start()
        return carry

    def so_far(h, which):
        return (
            rows_of(grad, h, core * 384 + yl * 192 + which * 96, 96)
            + rows_of(rc, h, yl * 192 + which * 96, 96)
            + rows_of(ry, h, which * 96, 96)
        )

    def y_stage(h, carry):
        ry_copy(h).wait_recv()
        s2[h] = so_far(h, 1 - zp).astype(jnp.bfloat16)
        rp_copy(h).start()
        return carry

    def pair_stage(h, carry):
        rp_copy(h).wait_recv()
        qb[pl.ds(pl.multiple_of(h * 96, 96), 96)] = (
            so_far(h, zp) + rp[h].astype(jnp.float32)
        ).astype(jnp.bfloat16)
        return carry

    def part_at(which):
        return pl.ds(pl.multiple_of(which * part, part), part)

    def rz_copy(i):
        other = (zo + i) % owners
        return remote(
            qb.at[part_at(other)],
            rz.at[zo],
            rz_send.at[other],
            rz_recv.at[zo],
            at_tok(z_peer(i)),
        )

    def rz_arrival(i):
        other = (zo + i) % owners
        return remote(
            qb.at[part_at(other)],
            rz.at[other],
            rz_send.at[other],
            rz_recv.at[other],
            at_tok(z_peer(i)),
        )

    pad_at = local_heads * 96
    qb[pl.ds(pad_at, EIGHTH - pad_at)] = jnp.zeros((EIGHTH - pad_at, dim), jnp.bfloat16)
    order = far_first(owners)

    here = core * 4 + yl * 2

    def shared(lane, which, send, recv, index, dev):
        piece = wsum.at[lane, part_at(which)]
        return remote(piece, piece, send.at[index], recv.at[index], at_tok(dev))

    def az_copy(i):
        piece = wsum.at[here + zp, part_at(zo)]
        return remote(
            piece, piece, az_send.at[(zo + i) % owners], az_recv.at[zo], at_tok(z_peer(i))
        )

    def az_arrival(i):
        other = (zo + i) % owners
        return shared(here + zp, other, az_send, az_recv, other, z_peer(i))

    def ap_copy(lane_pair, which):
        return shared(here + lane_pair, which, ap_send, ap_recv, which, pair)

    def ay_copy(lane_y, lane_pair, which):
        lane = core * 4 + lane_y * 2 + lane_pair
        return shared(lane, which, ay_send, ay_recv, lane_pair * owners + which, y_peer)

    def ac_copy(lane_core, lane_y, lane_pair, which):
        lane = lane_core * 4 + lane_y * 2 + lane_pair
        index = (lane_y * 2 + lane_pair) * owners + which
        return shared(lane, which, ac_send, ac_recv, index, partner)

    def ring(i):
        return (zo + i) % owners

    def arrived(slot):
        k_copy[slot].wait_recv()
        v_copy[slot].wait_recv()

    lax.fori_loop(0, local_heads, core_stage, 0)
    absorb(k_ref, v_ref, 0, first=True)
    lax.fori_loop(0, local_heads, y_stage, 0)
    for off in offsets:
        tot_copy(off).wait_recv()
    lax.fori_loop(0, local_heads, pair_stage, 0)
    for i in order:
        rz_copy(i).start()

    for slot in (1, 2):
        k_copy[slot].wait_recv()
    for slot in (0, 3, 4, 6):
        k_copy[slot].start()
    arrived(5)
    absorb_slot(5)
    for slot in (1, 2):
        v_copy[slot].wait_recv()
    for slot in (4, 6):
        v_copy[slot].start()
    absorb_slot(1)

    summed = qb[part_at(zo)].astype(jnp.float32)
    for i in order:
        rz_arrival(i).wait_recv()
        summed = summed + rz[ring(i)].astype(jnp.float32)
    wsum[here + zp, part_at(zo)] = summed.astype(jnp.bfloat16)
    for i in order:
        az_copy(i).start()
    ap_copy(zp, zo).start()
    ay_copy(yl, zp, zo).start()
    ac_copy(core, yl, zp, zo).start()
    for slot in (0, 3):
        v_copy[slot].start()

    absorb_slot(2)
    arrived(4)
    absorb_slot(4)

    for i in order:
        az_arrival(i).wait_recv()
        ap_copy(zp, ring(i)).start()
        ay_copy(yl, zp, ring(i)).start()
        ac_copy(core, yl, zp, ring(i)).start()
    for i in [0] + order:
        ap_copy(1 - zp, ring(i)).wait_recv()
        ay_copy(yl, 1 - zp, ring(i)).start()
        ac_copy(core, yl, 1 - zp, ring(i)).start()
    for lane_pair in (zp, 1 - zp):
        for i in [0] + order:
            ay_copy(1 - yl, lane_pair, ring(i)).wait_recv()
            ac_copy(core, 1 - yl, lane_pair, ring(i)).start()

    for slot in (0, 3):
        k_copy[slot].wait_recv()
    k_copy[7].start()
    arrived(6)
    absorb_slot(6)

    for lane_y in range(2):
        for lane_pair in range(2):
            for which in range(owners):
                ac_copy(1 - core, lane_y, lane_pair, which).wait_recv()

    def sums(h, first, size):
        pieces = []
        for piece in range(first // 32, (first + size) // 32):
            start = pl.multiple_of(h * 96 + (piece % 3) * 32, 32)
            pieces.append(wsum[piece // 3, pl.ds(start, 32)].astype(jnp.float32))
        return jnp.concatenate(pieces, axis=0)

    def renewed(h, base, first, size):
        base = base.astype(jnp.float32)
        updated = base - sums(h, first, size)
        norm = jnp.sqrt(jnp.sum(base * base, axis=0, keepdims=True))
        squares = jnp.sum(updated * updated, axis=0, keepdims=True)
        return (updated * (norm / jnp.sqrt(squares + epsilon))).astype(jnp.bfloat16)

    def apply_fast(h, carry):
        query_unit = qu[h]
        query_hidden = []
        for half in range(2):
            at = half * 128
            gate = dot(query_unit, renewed(h, fi_ref[h, :, at : at + 128], at, 128))
            lin = dot(
                query_unit,
                renewed(h, fi_ref[h, :, hid + at : hid + at + 128], 256 + at, 128),
            )
            query_hidden.append((silu_parts(gate)[1] * lin).astype(jnp.bfloat16))
        new_out = renewed(h, fo_ref[h], 512, hid)
        fast[h] = dot(jnp.concatenate(query_hidden, axis=1), new_out)
        return carry

    lax.fori_loop(0, local_heads, apply_fast, 0)

    for slot in (0, 3):
        v_copy[slot].wait_recv()
    v_copy[7].start()
    absorb_slot(0)
    absorb_slot(3)
    arrived(7)
    absorb_slot(7)

    def finish(h, carry):
        attended = jnp.transpose(acc[h] / l_ref[pl.ds(h, 1)])
        out_ref[h] = (attended + fast[h]).astype(jnp.bfloat16)
        return carry

    lax.fori_loop(0, local_heads, finish, 0)

    for i in range(1, n_head):
        ss_copy(i).wait_send()
    for off in offsets:
        tot_copy(off).wait_send()
    for slot in range(8):
        k_copy[slot].wait_send()
        v_copy[slot].wait_send()

    def sent(h, carry):
        rc_copy(h).wait_send()
        ry_copy(h).wait_send()
        rp_copy(h).wait_send()
        return carry

    lax.fori_loop(0, local_heads, sent, 0)
    for i in order:
        rz_copy(i).wait_send()
        az_copy(i).wait_send()
    for which in range(owners):
        ap_copy(zp, which).wait_send()
        for lane_pair in range(2):
            ay_copy(yl, lane_pair, which).wait_send()
            for lane_y in range(2):
                ac_copy(core, lane_y, lane_pair, which).wait_send()


def body(q, k, v, q_gain, k_gain, rate_in, rate_out, fast_in, fast_out, half_window, boundaries):
    rows, heads, dim = q.shape
    n_tok = lax.axis_size("tok")
    n_head = lax.axis_size("head")
    owners = n_tok // 8
    part = EIGHTH // owners
    bf16 = jnp.bfloat16
    f32 = jnp.float32
    vmem = pl.BlockSpec(memory_space=pltpu.VMEM)
    smem = pl.BlockSpec(memory_space=pltpu.SMEM)
    dma = pltpu.SemaphoreType.DMA

    def call(*refs):
        kernel(heads * n_head, n_tok, n_head, *refs)

    result = pl.pallas_call(
        call,
        out_shape=jax.ShapeDtypeStruct((heads, rows, dim), bf16),
        in_specs=[vmem] * 9 + [smem] * 2,
        out_specs=vmem,
        scratch_shapes=[
            pltpu.VMEM((8, heads, rows, dim), bf16),
            pltpu.VMEM((8, heads, rows, dim), bf16),
            pltpu.VMEM((8, rows), f32),
            pltpu.VMEM((n_head, 8, rows), f32),
            pltpu.VMEM((9, 8, rows), f32),
            pltpu.VMEM((heads, dim, rows), bf16),
            pltpu.VMEM((heads, rows, dim), bf16),
            pltpu.VMEM((8, rows), f32),
            pltpu.VMEM((8, rows), f32),
            pltpu.VMEM((heads, dim, rows), f32),
            pltpu.VMEM((heads, rows, 512), f32),
            pltpu.VMEM((heads, rows, dim), bf16),
            pltpu.VMEM((heads, rows, 256), f32),
            pltpu.VMEM((heads, HEAD_ROWS, dim), bf16),
            pltpu.VMEM((heads, HEAD_ROWS // 2, dim), bf16),
            pltpu.VMEM((heads, HEAD_ROWS // 4, dim), bf16),
            pltpu.VMEM((heads, HEAD_ROWS // 4, dim), bf16),
            pltpu.VMEM((heads, HEAD_ROWS // 8, dim), bf16),
            pltpu.VMEM((heads, HEAD_ROWS // 8, dim), bf16),
            pltpu.VMEM((EIGHTH, dim), bf16),
            pltpu.VMEM((owners, part, dim), bf16),
            pltpu.VMEM((8, EIGHTH, dim), bf16),
            pltpu.VMEM((heads, rows, dim), f32),
            dma((n_head,)),
            dma((n_head,)),
            dma((9,)),
            dma((9,)),
            dma((8,)),
            dma((8,)),
            dma((8,)),
            dma((8,)),
            dma((heads,)),
            dma((heads,)),
            dma((heads,)),
            dma((heads,)),
            dma((heads,)),
            dma((heads,)),
            dma((owners,)),
            dma((owners,)),
            dma((owners,)),
            dma((owners,)),
            dma((owners,)),
            dma((owners,)),
            dma((2 * owners,)),
            dma((2 * owners,)),
            dma((4 * owners,)),
            dma((4 * owners,)),
        ],
        compiler_params=pltpu.CompilerParams(
            collective_id=0, has_side_effects=True, vmem_limit_bytes=60 * 1024 * 1024
        ),
    )(
        jnp.transpose(q, (1, 0, 2)),
        jnp.transpose(k, (1, 0, 2)),
        jnp.transpose(v, (1, 0, 2)),
        q_gain,
        k_gain,
        rate_in,
        rate_out,
        fast_in,
        fast_out,
        half_window,
        boundaries,
    )
    return jnp.transpose(result, (1, 0, 2))


def solution(mesh):
    in_specs = (
        P("tok", "head", None),
        P("tok", "head", None),
        P("tok", "head", None),
        P("head", None),
        P("head", None),
        P("head", "tok"),
        P("head", "tok"),
        P("head", None, None),
        P("head", None, None),
        P("head"),
        P(),
    )
    out_specs = P("tok", "head", None)
    return jax.shard_map(body, mesh=mesh, in_specs=in_specs, out_specs=out_specs, check_vma=False)
```

time: 105 us -> 86.5 us (0.82); the launches traced: 103 us -> 85.6 us
  Pallas kernels: 101 us -> 83.9 us
    pallas_call x1, Pallas kernels: 101 us -> 83.9 us  [body(): pl.pallas_call(call, out_shape=jax.ShapeDtypeStruct((heads, rows, dim), b...]
where the time goes in v2:
time: 86.5 us; the launch traced here: 85.6 us
  Pallas kernels  83.9 us (97%)
  local copies, waits for them, and re-layouts  1.72 us (2%)
    pallas_call x1, Pallas kernels, body(): pl.pallas_call(call, out_shape=jax.ShapeDtypeStruct((heads, rows, dim), b...  83.9 us

profile of v2, /device:TPU:1, one launch (start us, length us, event | category | flops | bytes accessed | tf_op | source)
XLA Modules:
  0.0 85.6 jit_solution(17021264750493459292)
XLA Ops:
  0.0 83.9 %shard_map.109 = bf16[5,256,128]{2,1,0:T(8,128)(2,1)} custom-call(bf16[5,256,128]{2,1,0:T(8,128)(2,1)} %bitcast.5, bf16[5,256,128]{2,1,0:T(8,128)(2,1)} %bitcast.6, bf16[5,256,128]{2,1,0:T(8,128)(2,1)} %bitcast.7, f32[5,128]{1,0:T(8,128)} %refs_3_.1, f32[5,128]{1,0:T(8,128)} %refs_4_.1, f32[5,256]{1,0:T(8,128)} %refs_5_.1, f32[5,256]{1,0:T(8,128)} %refs_6_.1, ...), custom_call_target="tpu_custom_call" | custom-call | tf_op jit(solution)/shard_map/pallas_call | solution.py:594
  83.9 1.7 %copy.13 = bf16[256,5,128]{2,0,1:T(8,128)(2,1)} copy(bf16[256,5,128]{2,0,1:T(8,128)(2,1)} %bitcast.4) | data formatting | bytes 655360

commit v3 on v2

--- a/solution.py
+++ b/solution.py
@@ -35,6 +35,18 @@
     heads_all,
     n_tok,
     n_head,
+    q_hbm,
+    k_hbm,
+    v_hbm,
+    qg_hbm,
+    kg_hbm,
+    ri_hbm,
+    ro_hbm,
+    fi_hbm,
+    fo_hbm,
+    hw_ref,
+    bd_ref,
+    out_hbm,
     q_ref,
     k_ref,
     v_ref,
@@ -44,9 +56,9 @@
     ro_ref,
     fi_ref,
     fo_ref,
-    hw_ref,
-    bd_ref,
     out_ref,
+    in_sem,
+    out_sem,
     kh,
     vh,
     ss_loc,
@@ -94,6 +106,7 @@
     ay_recv,
     ac_send,
     ac_recv,
+    token,
 ):
     local_heads, rows, dim = k_ref.shape
     hid = fo_ref.shape[1]
@@ -108,14 +121,16 @@
     chip = t // 2
     z = chip % nz
     yl = chip // nz
-    zp = z % 2
-    zo = z // 2
+    shifted = (z + core) % nz
+    zp = shifted % 2
+    zo = shifted // 2
     partner = t + 1 - 2 * core
     y_peer = (1 - yl) * (2 * nz) + z * 2 + core
-    pair = yl * (2 * nz) + (z + 1 - 2 * zp) * 2 + core
+    pair = yl * (2 * nz) + ((z + 1 - 2 * zp + nz) % nz) * 2 + core
 
     def z_peer(i):
-        return yl * (2 * nz) + (((zo + i) % owners) * 2 + zp) * 2 + core
+        there = ((zo + i) % owners) * 2 + zp - core + nz
+        return yl * (2 * nz) + (there % nz) * 2 + core
 
     def tok_ring(off):
         return (t + off + n_tok) % n_tok
@@ -128,15 +143,31 @@
     def greet(dev):
         pl.semaphore_signal(barrier, inc=1, device_id=dev, device_id_type=MESH)
 
-    for i in far_first(owners):
-        greet(at_tok(z_peer(i)))
+    z_sides = sorted({1, owners - 1} - {0})
     for i in range(1, n_head):
         greet((t, (me_head + i) % n_head))
+    for i in z_sides:
+        greet(at_tok(z_peer(i)))
     for off in (1, 2, 3, 4):
         greet(at_tok(tok_ring(off)))
         greet(at_tok(tok_ring(-off)))
     greet(at_tok(y_peer))
     greet(at_tok(pair))
+
+    loads = []
+    for src, dst in (
+        (k_hbm, k_ref),
+        (q_hbm, q_ref),
+        (kg_hbm, kg_ref),
+        (fi_hbm, fi_ref),
+        (v_hbm, v_ref),
+        (ro_hbm, ro_ref),
+        (ri_hbm, ri_ref),
+        (fo_hbm, fo_ref),
+        (qg_hbm, qg_ref),
+    ):
+        loads.append(pltpu.make_async_copy(src, dst, in_sem.at[len(loads)]))
+        loads[-1].start()
 
     def remote(src, dst, send, recv, dev):
         return pltpu.make_async_remote_copy(
@@ -148,8 +179,27 @@
             device_id_type=MESH,
         )
 
+    pieces = ((0, 3), (3, local_heads - 3))
+
     def halo(ref, buf, send, recv, slot, dev):
-        return remote(ref, buf.at[slot], send.at[slot], recv.at[slot], at_tok(dev))
+        return [
+            remote(
+                ref.at[pl.ds(first, count)],
+                buf.at[slot, pl.ds(first, count)],
+                send.at[2 * slot + index],
+                recv.at[2 * slot + index],
+                at_tok(dev),
+            )
+            for index, (first, count) in enumerate(pieces)
+        ]
+
+    def start(copies, *which):
+        for index in which or (0, 1):
+            copies[index].start()
+
+    def wait_recv(copies):
+        for copy in copies:
+            copy.wait_recv()
 
     k_copy = {}
     v_copy = {}
@@ -174,6 +224,8 @@
 
     k_sq = jnp.zeros((rows, dim), jnp.float32)
     q_sq = jnp.zeros((rows, dim), jnp.float32)
+    loads[0].wait()
+    loads[1].wait()
     for h in range(local_heads):
         kf = k_ref[h].astype(jnp.float32)
         qf = q_ref[h].astype(jnp.float32)
@@ -186,7 +238,25 @@
         sub == 0, jnp.broadcast_to(k_row, (8, rows)), jnp.broadcast_to(q_row, (8, rows))
     )
 
-    pl.semaphore_wait(barrier, (owners - 1) + (n_head - 1) + 8 + 2)
+    pl.semaphore_wait(barrier, len(z_sides) + (n_head - 1) + 8 + 2)
+    rounds = max(owners // 2 - 1, 0)
+
+    def tokens_out(step):
+        if step < rounds:
+            for side, i in enumerate(z_sides):
+                pl.semaphore_signal(
+                    token.at[2 * step + side],
+                    inc=1,
+                    device_id=at_tok(z_peer(i)),
+                    device_id_type=MESH,
+                )
+
+    def tokens_in(step):
+        if step < rounds:
+            for side in range(len(z_sides)):
+                pl.semaphore_wait(token.at[2 * step + side], 1)
+
+    assert rounds <= 3
 
     def ss_copy(i):
         other = (me_head + i) % n_head
@@ -203,7 +273,11 @@
     for i in range(1, n_head):
         ss_copy(i).start()
     for slot in (1, 2, 5):
-        k_copy[slot].start()
+        start(k_copy[slot])
+    tokens_out(0)
+
+    for load in loads[2:]:
+        load.wait()
 
     def early(h, carry):
         key_gained = k_ref[h].astype(jnp.float32) * kg_ref[pl.ds(h, 1)]
@@ -234,8 +308,9 @@
     offsets = (1, -1, 2, -2, 3, -3, 4, -4)
     for off in offsets:
         tot_copy(off).start()
-    for slot in (1, 2, 5):
-        v_copy[slot].start()
+    for slot in (1, 2):
+        start(v_copy[slot], 0)
+    start(v_copy[5])
 
     inv_width = 1.0 / (heads_all * dim)
 
@@ -294,8 +369,6 @@
         qt[h] = jnp.transpose(raw * scaling).astype(jnp.bfloat16)
         qu[h] = unit(raw.astype(jnp.bfloat16))
         return carry
-
-    lax.fori_loop(0, local_heads, queries, 0)
 
     positions = t * rows + lax.broadcasted_iota(jnp.int32, (1, rows), 1)
     clip_first = jnp.zeros((1, rows), jnp.int32)
@@ -332,7 +405,7 @@
             acc[h] = product
             return carry
 
-        lax.fori_loop(0, local_heads, one, 0)
+        lax.fori_loop(0, local_heads, one, 0, unroll=True)
 
     def absorb_slot(slot):
         absorb(kh.at[slot], vh.at[slot], slot_off[slot])
@@ -438,29 +511,42 @@
         return (zo + i) % owners
 
     def arrived(slot):
-        k_copy[slot].wait_recv()
-        v_copy[slot].wait_recv()
+        wait_recv(k_copy[slot])
+        wait_recv(v_copy[slot])
 
     lax.fori_loop(0, local_heads, core_stage, 0)
+    tokens_in(0)
+    tokens_out(1)
+    lax.fori_loop(0, local_heads, queries, 0)
     absorb(k_ref, v_ref, 0, first=True)
+    tokens_in(1)
+    tokens_out(2)
     lax.fori_loop(0, local_heads, y_stage, 0)
+    for slot in (1, 2):
+        start(v_copy[slot], 1)
     for off in offsets:
         tot_copy(off).wait_recv()
+    arrived(5)
+    absorb_slot(5)
     lax.fori_loop(0, local_heads, pair_stage, 0)
+    tokens_in(2)
     for i in order:
         rz_copy(i).start()
 
     for slot in (1, 2):
-        k_copy[slot].wait_recv()
-    for slot in (0, 3, 4, 6):
-        k_copy[slot].start()
-    arrived(5)
-    absorb_slot(5)
+        wait_recv(k_copy[slot])
+    for slot in (0, 3):
+        start(k_copy[slot])
+    for slot in (4, 6):
+        start(k_copy[slot])
     for slot in (1, 2):
-        v_copy[slot].wait_recv()
+        wait_recv(v_copy[slot])
     for slot in (4, 6):
-        v_copy[slot].start()
+        start(v_copy[slot])
     absorb_slot(1)
+    absorb_slot(2)
+    arrived(4)
+    absorb_slot(4)
 
     summed = qb[part_at(zo)].astype(jnp.float32)
     for i in order:
@@ -473,32 +559,35 @@
     ay_copy(yl, zp, zo).start()
     ac_copy(core, yl, zp, zo).start()
     for slot in (0, 3):
-        v_copy[slot].start()
-
-    absorb_slot(2)
-    arrived(4)
-    absorb_slot(4)
+        start(v_copy[slot], 0)
+
+    arrived(6)
+    absorb_slot(6)
 
     for i in order:
         az_arrival(i).wait_recv()
         ap_copy(zp, ring(i)).start()
         ay_copy(yl, zp, ring(i)).start()
         ac_copy(core, yl, zp, ring(i)).start()
+    for slot in (0, 3):
+        start(v_copy[slot], 1)
     for i in [0] + order:
         ap_copy(1 - zp, ring(i)).wait_recv()
         ay_copy(yl, 1 - zp, ring(i)).start()
         ac_copy(core, yl, 1 - zp, ring(i)).start()
+    for slot in (0, 3):
+        wait_recv(k_copy[slot])
+    start(k_copy[7])
     for lane_pair in (zp, 1 - zp):
         for i in [0] + order:
             ay_copy(1 - yl, lane_pair, ring(i)).wait_recv()
             ac_copy(core, 1 - yl, lane_pair, ring(i)).start()
 
     for slot in (0, 3):
-        k_copy[slot].wait_recv()
-    k_copy[7].start()
-    arrived(6)
-    absorb_slot(6)
-
+        wait_recv(v_copy[slot])
+    start(v_copy[7])
+    absorb_slot(0)
+    absorb_slot(3)
     for lane_y in range(2):
         for lane_pair in range(2):
             for which in range(owners):
@@ -533,30 +622,26 @@
         fast[h] = dot(jnp.concatenate(query_hidden, axis=1), new_out)
         return carry
 
-    lax.fori_loop(0, local_heads, apply_fast, 0)
-
-    for slot in (0, 3):
-        v_copy[slot].wait_recv()
-    v_copy[7].start()
-    absorb_slot(0)
-    absorb_slot(3)
-    arrived(7)
-    absorb_slot(7)
-
     def finish(h, carry):
         attended = jnp.transpose(acc[h] / l_ref[pl.ds(h, 1)])
         out_ref[h] = (attended + fast[h]).astype(jnp.bfloat16)
         return carry
 
-    lax.fori_loop(0, local_heads, finish, 0)
+    def out_copy(h):
+        return pltpu.make_async_copy(out_ref.at[h], out_hbm.at[h], out_sem.at[h])
+
+    lax.fori_loop(0, local_heads, apply_fast, 0, unroll=True)
+    arrived(7)
+    absorb_slot(7)
+    lax.fori_loop(0, local_heads, finish, 0, unroll=True)
 
     for i in range(1, n_head):
         ss_copy(i).wait_send()
     for off in offsets:
         tot_copy(off).wait_send()
     for slot in range(8):
-        k_copy[slot].wait_send()
-        v_copy[slot].wait_send()
+        for copy in k_copy[slot] + v_copy[slot]:
+            copy.wait_send()
 
     def sent(h, carry):
         rc_copy(h).wait_send()
@@ -574,6 +659,10 @@
             ay_copy(yl, lane_pair, which).wait_send()
             for lane_y in range(2):
                 ac_copy(core, lane_y, lane_pair, which).wait_send()
+    for h in range(local_heads):
+        out_copy(h).start()
+    for h in range(local_heads):
+        out_copy(h).wait()
 
 
 def body(q, k, v, q_gain, k_gain, rate_in, rate_out, fast_in, fast_out, half_window, boundaries):
@@ -584,7 +673,7 @@
     part = EIGHTH // owners
     bf16 = jnp.bfloat16
     f32 = jnp.float32
-    vmem = pl.BlockSpec(memory_space=pltpu.VMEM)
+    hbm = pl.BlockSpec(memory_space=pl.ANY)
     smem = pl.BlockSpec(memory_space=pltpu.SMEM)
     dma = pltpu.SemaphoreType.DMA
 
@@ -594,9 +683,21 @@
     result = pl.pallas_call(
         call,
         out_shape=jax.ShapeDtypeStruct((heads, rows, dim), bf16),
-        in_specs=[vmem] * 9 + [smem] * 2,
-        out_specs=vmem,
+        in_specs=[hbm] * 9 + [smem] * 2,
+        out_specs=hbm,
         scratch_shapes=[
+            pltpu.VMEM((heads, rows, dim), bf16),
+            pltpu.VMEM((heads, rows, dim), bf16),
+            pltpu.VMEM((heads, rows, dim), bf16),
+            pltpu.VMEM((heads, dim), f32),
+            pltpu.VMEM((heads, dim), f32),
+            pltpu.VMEM((heads, rows), f32),
+            pltpu.VMEM((heads, rows), f32),
+            pltpu.VMEM((heads, dim, 512), bf16),
+            pltpu.VMEM((heads, 256, dim), bf16),
+            pltpu.VMEM((heads, rows, dim), bf16),
+            dma((9,)),
+            dma((heads,)),
             pltpu.VMEM((8, heads, rows, dim), bf16),
             pltpu.VMEM((8, heads, rows, dim), bf16),
             pltpu.VMEM((8, rows), f32),
@@ -624,10 +725,10 @@
             dma((n_head,)),
             dma((9,)),
             dma((9,)),
-            dma((8,)),
-            dma((8,)),
-            dma((8,)),
-            dma((8,)),
+            dma((16,)),
+            dma((16,)),
+            dma((16,)),
+            dma((16,)),
             dma((heads,)),
             dma((heads,)),
             dma((heads,)),
@@ -644,6 +745,7 @@
             dma((2 * owners,)),
             dma((4 * owners,)),
             dma((4 * owners,)),
+            pltpu.SemaphoreType.REGULAR((6,)),
         ],
         compiler_params=pltpu.CompilerParams(
             collective_id=0, has_side_effects=True, vmem_limit_bytes=60 * 1024 * 1024

time: 86.5 us -> 80.4 us (0.929)
  Pallas kernels: 83.9 us -> 78.5 us
    pallas_call x1, Pallas kernels: 83.9 us -> 78.5 us  [body(): pl.pallas_call(call, out_shape=jax.ShapeDtypeStruct((heads, rows, dim), b...]
where the time goes in v3:
time: 80.4 us; the launch traced here: 80.2 us
  Pallas kernels  78.5 us (98%)
  local copies, waits for them, and re-layouts  1.72 us (2%)
    pallas_call x1, Pallas kernels, body(): pl.pallas_call(call, out_shape=jax.ShapeDtypeStruct((heads, rows, dim), b...  78.5 us
    unnamed x1, local copies, waits for them, and re-layouts  1.72 us

profile of v3, /device:TPU:1, one launch (start us, length us, event | category | flops | bytes accessed | tf_op | source)
XLA Modules:
  0.0 80.2 jit_solution(6553344757940648211)
XLA Ops:
  0.0 78.5 %shard_map.109 = bf16[5,256,128]{2,1,0:T(8,128)(2,1)} custom-call(bf16[5,256,128]{2,1,0:T(8,128)(2,1)} %bitcast.5, bf16[5,256,128]{2,1,0:T(8,128)(2,1)} %bitcast.6, bf16[5,256,128]{2,1,0:T(8,128)(2,1)} %bitcast.7, f32[5,128]{1,0:T(8,128)} %refs_3_.1, f32[5,128]{1,0:T(8,128)} %refs_4_.1, f32[5,256]{1,0:T(8,128)} %refs_5_.1, f32[5,256]{1,0:T(8,128)} %refs_6_.1, ...), custom_call_target="tpu_custom_call" | custom-call | tf_op jit(solution)/shard_map/pallas_call | solution.py:683
  78.5 1.7 %copy.13 = bf16[256,5,128]{2,0,1:T(8,128)(2,1)} copy(bf16[256,5,128]{2,0,1:T(8,128)(2,1)} %bitcast.4) | data formatting | bytes 655360

commit v4 on v3

--- a/solution.py
+++ b/solution.py
@@ -378,7 +378,7 @@
         clip_first = jnp.where(positions >= edge, jnp.maximum(clip_first, edge), clip_first)
         clip_last = jnp.where(positions < edge, jnp.minimum(clip_last, edge - 1), clip_last)
 
-    def absorb(keys, values, off, first=False):
+    def absorb(keys, values, off, first=False, which=None):
         scale = k_scale if first else scale_of(tot_all[off + 4][0:1])
         places = (t + off) * rows + lax.broadcasted_iota(jnp.int32, (rows, rows), 0)
 
@@ -405,10 +405,11 @@
             acc[h] = product
             return carry
 
-        lax.fori_loop(0, local_heads, one, 0, unroll=True)
-
-    def absorb_slot(slot):
-        absorb(kh.at[slot], vh.at[slot], slot_off[slot])
+        low_head, count = (0, local_heads) if which is None else pieces[which]
+        lax.fori_loop(low_head, low_head + count, one, 0, unroll=True)
+
+    def absorb_slot(slot, which=None):
+        absorb(kh.at[slot], vh.at[slot], slot_off[slot], which=which)
 
     def arrived(slot):
         k_copy[slot].wait_recv()
@@ -578,16 +579,24 @@
     for slot in (0, 3):
         wait_recv(k_copy[slot])
     start(k_copy[7])
+    for slot in (0, 3):
+        v_copy[slot][0].wait_recv()
+    start(v_copy[7], 0)
+    absorb_slot(0, 0)
+    absorb_slot(3, 0)
     for lane_pair in (zp, 1 - zp):
         for i in [0] + order:
             ay_copy(1 - yl, lane_pair, ring(i)).wait_recv()
             ac_copy(core, 1 - yl, lane_pair, ring(i)).start()
 
+    wait_recv(k_copy[7])
+    v_copy[7][0].wait_recv()
+    absorb_slot(7, 0)
     for slot in (0, 3):
-        wait_recv(v_copy[slot])
-    start(v_copy[7])
-    absorb_slot(0)
-    absorb_slot(3)
+        v_copy[slot][1].wait_recv()
+    start(v_copy[7], 1)
+    absorb_slot(0, 1)
+    absorb_slot(3, 1)
     for lane_y in range(2):
         for lane_pair in range(2):
             for which in range(owners):
@@ -631,8 +640,8 @@
         return pltpu.make_async_copy(out_ref.at[h], out_hbm.at[h], out_sem.at[h])
 
     lax.fori_loop(0, local_heads, apply_fast, 0, unroll=True)
-    arrived(7)
-    absorb_slot(7)
+    v_copy[7][1].wait_recv()
+    absorb_slot(7, 1)
     lax.fori_loop(0, local_heads, finish, 0, unroll=True)
 
     for i in range(1, n_head):

time: 80.4 us -> 78.9 us (0.981)
  Pallas kernels: 78.5 us -> 77 us
    pallas_call x1, Pallas kernels: 78.5 us -> 77 us  [body(): pl.pallas_call(call, out_shape=jax.ShapeDtypeStruct((heads, rows, dim), b...]
where the time goes in v4:
time: 78.9 us; the launch traced here: 78.7 us
  Pallas kernels  77 us (98%)
  local copies, waits for them, and re-layouts  1.72 us (2%)
    pallas_call x1, Pallas kernels, body(): pl.pallas_call(call, out_shape=jax.ShapeDtypeStruct((heads, rows, dim), b...  77 us
    unnamed x1, local copies, waits for them, and re-layouts  1.72 us

profile of v4, /device:TPU:1, one launch (start us, length us, event | category | flops | bytes accessed | tf_op | source)
XLA Modules:
  0.0 78.7 jit_solution(10869007488520294618)
XLA Ops:
  0.0 77.0 %shard_map.109 = bf16[5,256,128]{2,1,0:T(8,128)(2,1)} custom-call(bf16[5,256,128]{2,1,0:T(8,128)(2,1)} %bitcast.5, bf16[5,256,128]{2,1,0:T(8,128)(2,1)} %bitcast.6, bf16[5,256,128]{2,1,0:T(8,128)(2,1)} %bitcast.7, f32[5,128]{1,0:T(8,128)} %refs_3_.1, f32[5,128]{1,0:T(8,128)} %refs_4_.1, f32[5,256]{1,0:T(8,128)} %refs_5_.1, f32[5,256]{1,0:T(8,128)} %refs_6_.1, ...), custom_call_target="tpu_custom_call" | custom-call | tf_op jit(solution)/shard_map/pallas_call | solution.py:692
  77.0 1.7 %copy.13 = bf16[256,5,128]{2,0,1:T(8,128)(2,1)} copy(bf16[256,5,128]{2,0,1:T(8,128)(2,1)} %bitcast.4) | data formatting | bytes 655360
